TPU v7x, 32 devices: a whole 2x2x4 slice. The times are simulated.
32 devices in a mesh: parts: 2 (over x), harm: 4 (over y, core), tile: 4 (over z).
Axes of the slice: x: 2, y: 2, z: 4, core: 2. Of those that a mesh axis runs over, the one named last changes fastest.
Arguments:
- perturbation: float32 [8, 2, 5, 128, 256], P('harm', None, None, ('parts', 'tile')), parts along dimension 3, may hold values from -6 to 6
- base_flow: float32 [8, 2, 3, 128, 256], P('harm', None, None, ('parts', 'tile')), parts along dimension 3, may hold values from -0.9 to 0.9
- viscosity: float32 [128, 256], P(('parts', 'tile')), parts along dimension 0, may hold values from 0.05 to 0.5
Outputs:
- resolvent_image: float32 [8, 2, 5, 128, 256], P('harm', None, None, ('parts', 'tile')), parts along dimension 3
There are 2 independent parts, one for each index of `parts`. A program takes and returns all parts, laid end to end along the dimension named above; each array names one. Nothing has to cross between parts.
All inputs are finite; a program needn't handle non-finite values.
Results may differ from a plain program's by a relative error of at most 0.00002.
Values sent between devices are 32-bit elements; how exact they have to be, the bound alone decides.
A program may use at most 64 MiB of HBM per device.

v0:
```python
import jax
import jax.numpy as jnp
import numpy as np
from jax import lax
from jax.sharding import PartitionSpec as P

omega_base = 0.25


def extended(cells, sides, width):
    for axis, dim in sides:
        count = lax.axis_size(axis)
        head = lax.slice_in_dim(cells, 0, width, axis=dim)
        tail = lax.slice_in_dim(cells, cells.shape[dim] - width, cells.shape[dim], axis=dim)
        cells = jnp.concatenate(
            [
                lax.ppermute(tail, axis, [(i, (i + 1) % count) for i in range(count)]),
                cells,
                lax.ppermute(head, axis, [((i + 1) % count, i) for i in range(count)]),
            ],
            axis=dim,
        )
    return cells


def shifted(value, axis, steps):
    count = lax.axis_size(axis)
    pairs = [(source, (source + steps) % count) for source in range(count)]
    return lax.ppermute(value, axis, pairs)


def split_rows(padded):
    middle = padded[..., 1:-1, :]
    grad_x = 0.5 * (padded[..., 2:, :] - padded[..., :-2, :])
    grad_y = 0.5 * (jnp.roll(middle, -1, -1) - jnp.roll(middle, 1, -1))
    return (middle, grad_x, grad_y)


def diffusion(padded, visc_padded):
    middle = padded[..., 1:-1, :]
    center = visc_padded[1:-1]
    east_face = 0.5 * (center + visc_padded[2:])
    west_face = 0.5 * (center + visc_padded[:-2])
    north_face = 0.5 * (center + jnp.roll(center, -1, -1))
    south_face = 0.5 * (center + jnp.roll(center, 1, -1))
    return (
        east_face * (padded[..., 2:, :] - middle)
        - west_face * (middle - padded[..., :-2, :])
        + north_face * (jnp.roll(middle, -1, -1) - middle)
        - south_face * (middle - jnp.roll(middle, 1, -1))
    )


def acoustic(grad_x, grad_y):
    dilation = grad_x[..., 1, :, :] + grad_y[..., 2, :, :]
    return jnp.stack(
        [dilation, grad_x[..., 4, :, :], grad_y[..., 4, :, :], jnp.zeros_like(dilation), dilation],
        axis=-3,
    )


def own_terms(middle, grad_x, grad_y, damping, frequency):
    rotation = jnp.stack([-frequency * middle[:, 1], frequency * middle[:, 0]], axis=1)
    return rotation + acoustic(grad_x, grad_y) - damping


def coupling(
    u_real, u_imag, v_real, v_imag, g_real, g_imag, q_real, q_imag, x_real, x_imag, y_real, y_imag
):
    real_part = (
        u_real * x_real
        - u_imag * x_imag
        + v_real * y_real
        - v_imag * y_imag
        + g_real * q_real
        - g_imag * q_imag
    )
    imag_part = (
        u_real * x_imag
        + u_imag * x_real
        + v_real * y_imag
        + v_imag * y_real
        + g_real * q_imag
        + g_imag * q_real
    )
    return (real_part, imag_part)


def block_terms(blocks, middle, grad_x, grad_y):
    local_count = middle.shape[0]
    index_table = np.array(
        [
            [local_count + target - source for source in range(local_count)]
            for target in range(local_count)
        ],
        dtype=np.int32,
    )
    chosen = blocks[index_table]

    def base_part(complex_index, field_index):
        return chosen[:, :, complex_index, field_index][:, :, None]

    def moved_part(values, complex_index):
        return values[None, :, complex_index]

    real_part, imag_part = coupling(
        base_part(0, 0),
        base_part(1, 0),
        base_part(0, 1),
        base_part(1, 1),
        base_part(0, 2),
        base_part(1, 2),
        moved_part(middle, 0),
        moved_part(middle, 1),
        moved_part(grad_x, 0),
        moved_part(grad_x, 1),
        moved_part(grad_y, 0),
        moved_part(grad_y, 1),
    )
    return jnp.stack([jnp.sum(real_part, axis=1), jnp.sum(imag_part, axis=1)], axis=1)


def shards(perturbation, base_flow, viscosity):
    local_count = perturbation.shape[0]
    width_x = perturbation.shape[3]
    width_y = perturbation.shape[4]
    groups = lax.axis_size("harm")
    first_index = lax.axis_index("harm") * local_count
    flattened = perturbation.reshape(local_count * 10, width_x, width_y)
    stacked = jnp.concatenate([flattened, viscosity[None]], axis=0)
    padded = extended(stacked, (("tile", 1),), 1)
    own_padded = padded[:-1].reshape(local_count, 2, 5, width_x + 2, width_y)
    visc_padded = padded[-1]
    numbers = first_index + jnp.arange(local_count, dtype=jnp.int32)
    total_count = local_count * groups
    signed = jnp.where(numbers < total_count // 2, numbers, numbers - total_count)
    frequency = (omega_base * signed.astype(jnp.float32)).reshape(local_count, 1, 1, 1)
    middle, grad_x, grad_y = split_rows(own_padded)
    summed = own_terms(middle, grad_x, grad_y, diffusion(own_padded, visc_padded), frequency)
    whole_base = lax.all_gather(base_flow, "harm", axis=0, tiled=True)

    def base_pair(position, earlier):
        before = lax.dynamic_slice_in_dim(
            whole_base, (position + groups - 1) % groups * local_count, local_count, 0
        )
        current = lax.dynamic_slice_in_dim(whole_base, position * local_count, local_count, 0)
        return (jnp.concatenate([before, current], axis=0), earlier)

    earlier = base_flow
    moving = own_padded

    def advance(moving):
        moved = shifted(moving, "harm", 1)
        return (moved, moved)

    blocks, earlier = base_pair(0, earlier)
    summed = summed + block_terms(blocks, middle, grad_x, grad_y)

    def advance_step(position, carried):
        summed, moving, earlier = carried
        moving, rimmed = advance(moving)
        blocks, earlier = base_pair(position, earlier)
        values, slope_x, slope_y = split_rows(rimmed)
        return (summed + block_terms(blocks, values, slope_x, slope_y), moving, earlier)

    summed, moving, earlier = lax.fori_loop(1, groups, advance_step, (summed, moving, earlier))
    return summed


def solution(mesh):
    placed = (
        P("harm", None, None, ("parts", "tile"), None),
        P("harm", None, None, ("parts", "tile"), None),
        P(("parts", "tile"), None),
    )
    return jax.shard_map(
        shards,
        mesh=mesh,
        in_specs=placed,
        out_specs=P("harm", None, None, ("parts", "tile"), None),
        check_vma=False,
    )
```

profile of v0, /device:TPU:0, one launch (start us, length us, event | category | flops | bytes accessed | tf_op | source)
XLA Modules:
  0.0 47.7 jit_solution(18082950959541213090)
XLA Ops:
  0.0 1.1 %pad_maximum_fusion.8 = (f32[21,1,256]{2,1,0:T(1,128)S(1)}, f32[21,1,256]{2,1,0:T(1,128)S(1)}) fusion(f32[1,16,256]{2,1,0:T(8,128)} %bitcast.94, f32[20,16,256]{2,1,0:T(8,128)} %bitcast.90), kind=kLoop, calls=%fused_computation.57 | loop fusion | flops 10752 | bytes 387072 | tf_op jit(solution)/shard_map/slice | solution.py:14
  1.1 5.1 %collective-permute-start.2 = (f32[21,1,256]{2,1,0:T(1,128)S(1)}, f32[21,1,256]{2,1,0:T(1,128)S(1)}, u32[]{:S(2)}, u32[]{:S(2)}) collective-permute-start(f32[21,1,256]{2,1,0:T(1,128)S(1)} %get-tuple-element.304), channel_id=1, source_target_pairs={{1,0},{2,1},{3,2},{0,3},{5,4},{6,5},{7,6},{4,7},{9,8},{10,9},{11,1... | collective-permute-start | bytes 64520 | tf_op jit(solution)/shard_map/ppermute | solution.py:19
  6.2 0.0 collective-permute-start.1
  6.2 0.1 fusion.23
  6.3 0.1 fusion.22
  6.4 8.6 %all_gather.3 = f32[8,2,3,16,256]{4,3,2,1,0:T(8,128)S(1)} all-gather(f32[2,2,3,16,256]{4,3,2,1,0:T(8,128)S(1)} %copy-done.2), channel_id=1, replica_groups=mesh['parts'=2,'harm'=4,'tile'=4] {'harm'}, dimensions={0}, use_global_device_ids=true | all-gather | bytes 983040 | tf_op jit(solution)/shard_map/all_gather | solution.py:140
  15.0 0.6 %copy-done.3 = s32[4]{0:T(128)S(1)} copy-done((s32[4]{0:T(128)S(1)}, s32[4]{0:T(128)}, u32[]{:S(2)}) %copy-start.3) | copy-done | bytes 40
  15.7 0.6 %gather_fusion.1 = f32[4,2,3,16,256]{4,3,2,1,0:T(8,128)S(1)} fusion(f32[4,2,3,16,256]{4,3,2,1,0:T(8,128)S(1)} %pad_maximum_fusion.4, s32[1024]{0:T(1024)S(1)} %pad_clamp_fusion.1), kind=kCustom, calls=%fused_computation.1 | custom fusion | bytes 786448 | tf_op jit(solution)/shard_map/gather | solution.py:98
  16.3 0.0 copy-start
  16.3 0.0 collective-permute-done.2
  16.4 0.9 %copy-done = f32[2,2,5,16,256]{4,3,2,1,0:T(8,128)S(1)} copy-done((f32[2,2,5,16,256]{4,3,2,1,0:T(8,128)S(1)}, f32[2,2,5,16,256]{4,3,2,1,0:T(8,128)}, u32[]{:S(2)}) %copy-start) | copy-done | bytes 327704
  17.3 0.1 pad_maximum_fusion.1
  17.3 0.2 fusion.20
  17.5 0.1 fusion.21
  17.6 0.2 subtract_multiply_fusion
  18.0 0.1 slice_bitcast_fusion.16
  18.1 0.3 subtract_reduce_fusion.1
  18.4 0.1 fusion.11
  18.5 0.3 fusion.3
  18.8 28.2 %while.21 = (s32[]{:T(128)}, f32[2,2,5,16,256]{4,3,2,0,1:T(8,128)S(1)}, f32[2,2,5,18,256]{4,3,2,0,1:T(8,128)S(1)}, f32[8,2,3,16,256]{4,3,2,1,0:T(8,128)S(1)}, s3...) while((s32[]{:T(128)}, ...), condition=%wide.region_5.6_spmd.clone, body=%wide.region_2.5_spmd.sunk.clone.sunk | while | flops 2638870 | bytes 13291922 | solution.py:166
  18.8 0.4 collective-permute-start
  19.3 0.6 %gather_fusion = f32[4,2,3,16,256]{4,3,2,1,0:T(8,128)S(1)} fusion(f32[4,2,3,16,256]{4,3,2,1,0:T(8,128)S(1)} %pad_maximum_fusion.14, s32[1024]{0:T(1024)S(1)} %pad_clamp_fusion.3), kind=kCustom, calls=%fused_computation.clone.1 | custom fusion | bytes 786448 | tf_op jit(solution)/shard_map/while/body/eval_jaxpr/gather | solution.py:98
  19.9 7.2 %collective-permute-done = f32[2,2,5,18,256]{4,3,2,0,1:T(8,128)S(1)} collective-permute-done((f32[2,2,5,18,256]{4,3,2,0,1:T(8,128)S(1)}, f32[2,2,5,18,256]{4,3,2,0,1:T(8,128)S(1)}, u32[]{:S(2)}, u32[]{:S(2)}) %collective-permute-start) | collective-permute-done | bytes 368672 | tf_op jit(solution)/shard_map/while/body/eval_jaxpr/ppermute | solution.py:29
  27.2 0.1 fusion.33
  27.3 0.2 fusion.34
  27.5 0.2 fusion.35
  27.7 0.1 slice_bitcast_fusion.27
  27.8 0.3 subtract_reduce_fusion.3
  28.0 0.1 maximum_add_fusion.5
  28.2 0.1 collective-permute-start
  28.4 0.6 %gather_fusion = f32[4,2,3,16,256]{4,3,2,1,0:T(8,128)S(1)} fusion(f32[4,2,3,16,256]{4,3,2,1,0:T(8,128)S(1)} %pad_maximum_fusion.14, s32[1024]{0:T(1024)S(1)} %pad_clamp_fusion.3), kind=kCustom, calls=%fused_computation.clone.1 | custom fusion | bytes 786448 | tf_op jit(solution)/shard_map/while/body/eval_jaxpr/gather | solution.py:98
  29.0 7.5 %collective-permute-done = f32[2,2,5,18,256]{4,3,2,0,1:T(8,128)S(1)} collective-permute-done((f32[2,2,5,18,256]{4,3,2,0,1:T(8,128)S(1)}, f32[2,2,5,18,256]{4,3,2,0,1:T(8,128)S(1)}, u32[]{:S(2)}, u32[]{:S(2)}) %collective-permute-start) | collective-permute-done | bytes 368672 | tf_op jit(solution)/shard_map/while/body/eval_jaxpr/ppermute | solution.py:29
  36.6 0.1 fusion.33
  36.7 0.2 fusion.34
  36.9 0.2 fusion.35
  37.1 0.1 slice_bitcast_fusion.27
  37.2 0.3 subtract_reduce_fusion.3
  37.4 0.1 maximum_add_fusion.5
  37.6 0.1 collective-permute-start
  37.8 0.6 %gather_fusion = f32[4,2,3,16,256]{4,3,2,1,0:T(8,128)S(1)} fusion(f32[4,2,3,16,256]{4,3,2,1,0:T(8,128)S(1)} %pad_maximum_fusion.14, s32[1024]{0:T(1024)S(1)} %pad_clamp_fusion.3), kind=kCustom, calls=%fused_computation.clone.1 | custom fusion | bytes 786448 | tf_op jit(solution)/shard_map/while/body/eval_jaxpr/gather | solution.py:98
  38.4 7.5 %collective-permute-done = f32[2,2,5,18,256]{4,3,2,0,1:T(8,128)S(1)} collective-permute-done((f32[2,2,5,18,256]{4,3,2,0,1:T(8,128)S(1)}, f32[2,2,5,18,256]{4,3,2,0,1:T(8,128)S(1)}, u32[]{:S(2)}, u32[]{:S(2)}) %collective-permute-start) | collective-permute-done | bytes 368672 | tf_op jit(solution)/shard_map/while/body/eval_jaxpr/ppermute | solution.py:29
  46.0 0.1 fusion.33
  46.1 0.2 fusion.34
  46.3 0.2 fusion.35
  46.5 0.1 slice_bitcast_fusion.27
  46.5 0.3 subtract_reduce_fusion.3
  46.8 0.1 maximum_add_fusion.5
  47.0 0.7 %copy.19 = f32[2,2,5,16,256]{4,3,2,1,0:T(8,128)} copy(f32[2,2,5,16,256]{4,3,2,0,1:T(8,128)S(1)} %get-tuple-element.231) | data formatting | bytes 655360 | tf_op jit(solution)/shard_map/while | solution.py:166
  (40 shorter events, 0.8 us)
Async XLA Ops:
  0.0 6.2 %copy-start.1 = (f32[16,256]{1,0:T(8,128)S(1)}, f32[16,256]{1,0:T(8,128)}, u32[]{:S(2)}) copy-start(f32[16,256]{1,0:T(8,128)} %param.11) | copy-start | bytes 49156
  0.0 6.4 %copy-start.2 = (f32[2,2,3,16,256]{4,3,2,1,0:T(8,128)S(1)}, f32[2,2,3,16,256]{4,3,2,1,0:T(8,128)}, u32[]{:S(2)}) copy-start(f32[2,2,3,16,256]{4,3,2,1,0:T(8,128)} %param.10) | copy-start | bytes 589828
  1.1 15.2 %collective-permute-start.2 = (f32[21,1,256]{2,1,0:T(1,128)S(1)}, f32[21,1,256]{2,1,0:T(1,128)S(1)}, u32[]{:S(2)}, u32[]{:S(2)}) collective-permute-start(f32[21,1,256]{2,1,0:T(1,128)S(1)} %get-tuple-element.304), channel_id=1, source_target_pairs={{1,0},{2,1},{3,2},{0,3},{5,4},{6,5},{7,6},{4,7},{9,8},{10,9},{11,1... | collective-permute-start | bytes 64520 | tf_op jit(solution)/shard_map/ppermute | solution.py:19
  6.2 10.1 %collective-permute-start.1 = (f32[21,1,256]{2,1,0:T(1,128)S(1)}, f32[21,1,256]{2,1,0:T(1,128)S(1)}, u32[]{:S(2)}, u32[]{:S(2)}) collective-permute-start(f32[21,1,256]{2,1,0:T(1,128)S(1)} %get-tuple-element.303), channel_id=1, source_target_pairs={{0,1},{1,2},{2,3},{3,0},{4,5},{5,6},{6,7},{7,4},{8,9},{9,10},{10,1... | collective-permute-start | bytes 64520 | tf_op jit(solution)/shard_map/ppermute | solution.py:17
  15.0 0.7 %copy-start.3 = (s32[4]{0:T(128)S(1)}, s32[4]{0:T(128)}, u32[]{:S(2)}) copy-start(s32[4]{0:T(128)} %constant.163) | copy-start | bytes 52
  16.3 1.0 %copy-start = (f32[2,2,5,16,256]{4,3,2,1,0:T(8,128)S(1)}, f32[2,2,5,16,256]{4,3,2,1,0:T(8,128)}, u32[]{:S(2)}) copy-start(f32[2,2,5,16,256]{4,3,2,1,0:T(8,128)} %param.9) | copy-start | bytes 983044
  18.8 8.3 %collective-permute-start = (f32[2,2,5,18,256]{4,3,2,0,1:T(8,128)S(1)}, f32[2,2,5,18,256]{4,3,2,0,1:T(8,128)S(1)}, u32[]{:S(2)}, u32[]{:S(2)}) collective-permute-start(f32[2,2,5,18,256]{4,3,2,0,1:T(8,128)S(1)} %get-tuple-element.397), channel_id=1, source_target_pairs={{0,4},{4,8},{8,12},{12,0},{1,5},{5,9},{9,13},{13,1},{2,6},{6,10},{... | collective-permute-start | bytes 1105928 | tf_op jit(solution)/shard_map/while/body/eval_jaxpr/ppermute | solution.py:29
  28.2 8.3 %collective-permute-start = (f32[2,2,5,18,256]{4,3,2,0,1:T(8,128)S(1)}, f32[2,2,5,18,256]{4,3,2,0,1:T(8,128)S(1)}, u32[]{:S(2)}, u32[]{:S(2)}) collective-permute-start(f32[2,2,5,18,256]{4,3,2,0,1:T(8,128)S(1)} %get-tuple-element.397), channel_id=1, source_target_pairs={{0,4},{4,8},{8,12},{12,0},{1,5},{5,9},{9,13},{13,1},{2,6},{6,10},{... | collective-permute-start | bytes 1105928 | tf_op jit(solution)/shard_map/while/body/eval_jaxpr/ppermute | solution.py:29
  37.6 8.3 %collective-permute-start = (f32[2,2,5,18,256]{4,3,2,0,1:T(8,128)S(1)}, f32[2,2,5,18,256]{4,3,2,0,1:T(8,128)S(1)}, u32[]{:S(2)}, u32[]{:S(2)}) collective-permute-start(f32[2,2,5,18,256]{4,3,2,0,1:T(8,128)S(1)} %get-tuple-element.397), channel_id=1, source_target_pairs={{0,4},{4,8},{8,12},{12,0},{1,5},{5,9},{9,13},{13,1},{2,6},{6,10},{... | collective-permute-start | bytes 1105928 | tf_op jit(solution)/shard_map/while/body/eval_jaxpr/ppermute | solution.py:29
where the time goes:
time: 47.9 us; the launch traced here: 47.7 us
  waiting for transfers between devices  22.2 us (46%)
  blocking collectives  8.61 us (18%)
  local copies, waits for them, and re-layouts  6.52 us (14%)
  starting transfers between devices  5.65 us (12%)
  other arithmetic  4.13 us (9%)
    ppermute x3, waiting for transfers between devices, shifted(): return lax.ppermute(value, axis, pairs)  22.2 us
    all_gather x1, blocking collectives, shards(): whole_base = lax.all_gather(base_flow, 'harm', axis=0, tiled=True)  8.61 us
    ppermute x1, starting transfers between devices, extended(): lax.ppermute(head, axis, [((i + 1) % count, i) for i in range(count)])  5.13 us
    gather x4, local copies, waits for them, and re-layouts, block_terms(): chosen = blocks[index_table]  2.3 us
    unnamed x11, local copies, waits for them, and re-layouts  1.54 us
    reduce_sum x4, other arithmetic, block_terms(): jnp.sum(real_part, axis=1)  1.12 us
    slice x1, other arithmetic, extended(): lax.slice_in_dim(cells, cells.shape[dim] - width, cells.shape[dim], axis=...  1.1 us
    slice x8, local copies, waits for them, and re-layouts, split_rows(): grad_y = 0.5 * (jnp.roll(middle, -1, -1) - jnp.roll(middle, 1, -1))  1.09 us
  transfers between devices with their start and end apart: 5, of which 3 were waited for; matrix products, arithmetic and copies ran while one was open for 6% of the time, Pallas kernels for 0%

commit v1 on v0

v1 whole, which is shorter than its diff:
```python
import functools

import jax
import jax.numpy as jnp
from jax import lax
from jax.experimental import pallas as pl
from jax.experimental.pallas import tpu as pltpu
from jax.sharding import PartitionSpec as P

omega_base = 0.25
MESH = pl.DeviceIdType.MESH


def kernel(
    groups,
    tiles,
    p_hbm,
    b_hbm,
    v_hbm,
    out,
    pbuf,
    bbuf,
    vbuf,
    stage,
    rims,
    gx,
    gy,
    local_sem,
    y_send,
    y_recv,
    chip_send,
    chip_recv,
    z_send,
    z_recv,
    rim_send,
    rim_recv,
):
    local, _, fields, rows, width = p_hbm.shape
    total = pbuf.shape[0]
    cores = 2
    chips = groups // cores
    rim_rows = local * 2 * fields
    me = lax.axis_index("harm")
    chip, core = me // cores, me % cores
    place = lax.axis_index("tile")
    partner = chip * cores + (1 - core)
    above, below = (place + 1) % tiles, (place + tiles - 1) % tiles

    def group_at(distance, own_core):
        at = (chip + chips - distance) % chips
        return at * cores + (core if own_core else 1 - core)

    def target_at(distance):
        return (chip + distance) % chips * cores + core

    first = me * local

    copy_p = pltpu.make_async_copy(p_hbm, pbuf.at[pl.ds(first, local)], local_sem.at[0])
    copy_b = pltpu.make_async_copy(b_hbm, bbuf.at[pl.ds(first, local)], local_sem.at[1])
    copy_v = pltpu.make_async_copy(v_hbm, vbuf, local_sem.at[2])
    copy_p.start()
    copy_v.start()
    copy_b.start()

    barrier = pltpu.get_barrier_semaphore()
    for distance in range(1, chips):
        pl.semaphore_signal(
            barrier, inc=1, device_id={"harm": target_at(distance)}, device_id_type=MESH
        )
    pl.semaphore_signal(barrier, inc=1, device_id={"harm": partner}, device_id_type=MESH)
    pl.semaphore_signal(barrier, inc=1, device_id={"tile": above}, device_id_type=MESH)
    pl.semaphore_signal(barrier, inc=1, device_id={"tile": below}, device_id_type=MESH)

    def pack(distance):
        start = group_at(distance, True) * local
        for index in range(local):
            for part in range(2):
                for field in range(fields):
                    row = (index * 2 + part) * fields + field
                    stage[distance, 0, row : row + 1, :] = pbuf[start + index, part, field, 0:1, :]
                    stage[distance, 1, row : row + 1, :] = pbuf[
                        start + index, part, field, rows - 1 : rows, :
                    ]

    copy_p.wait()
    copy_v.wait()
    pack(0)
    stage[0, 0, rim_rows : rim_rows + 1, :] = vbuf[0:1, :]
    stage[0, 1, rim_rows : rim_rows + 1, :] = vbuf[rows - 1 : rows, :]

    pl.semaphore_wait(barrier, chips + 2)

    y_copies = []
    for kind in range(2):
        source, dest = ((p_hbm, pbuf), (b_hbm, bbuf))[kind]
        for index in range(local):
            for distance in range(1, chips):
                copy = pltpu.make_async_remote_copy(
                    src_ref=source.at[index],
                    dst_ref=dest.at[first + index],
                    send_sem=y_send.at[distance - 1, kind, index],
                    recv_sem=y_recv.at[distance - 1, kind, index],
                    device_id={"harm": target_at(distance)},
                    device_id_type=MESH,
                )
                copy.start()
                y_copies.append((distance, kind, index, copy))

    def rim_copies(distance):
        group = group_at(distance, True)
        return [
            pltpu.make_async_remote_copy(
                src_ref=stage.at[distance, side],
                dst_ref=rims.at[group, 1 - side],
                send_sem=z_send.at[distance, side],
                recv_sem=z_recv.at[distance, side],
                device_id={"tile": (below, above)[side]},
                device_id_type=MESH,
            )
            for side in range(2)
        ]

    started = []
    rim_pending = {}

    def send_rims(distance):
        rim_pending[distance] = rim_copies(distance)
        for copy in rim_pending[distance]:
            copy.start()

    def relay_copy(distance, kind, index):
        at = group_at(distance, True) * local + index
        dest = (pbuf, bbuf)[kind]
        source = dest.at[at] if distance else (p_hbm, b_hbm)[kind].at[index]
        return pltpu.make_async_remote_copy(
            src_ref=source,
            dst_ref=dest.at[at],
            send_sem=chip_send.at[distance, kind, index],
            recv_sem=chip_recv.at[distance, kind, index],
            device_id={"harm": partner},
            device_id_type=MESH,
        )

    relays = {}

    def relay(distance, kind, index):
        relays[distance, kind, index] = relay_copy(distance, kind, index)
        relays[distance, kind, index].start()

    def relay_rims(distance):
        group = group_at(distance, True)
        relays[distance] = pltpu.make_async_remote_copy(
            src_ref=rims.at[group],
            dst_ref=rims.at[group],
            send_sem=rim_send.at[distance],
            recv_sem=rim_recv.at[distance],
            device_id={"harm": partner},
            device_id_type=MESH,
        )
        relays[distance].start()

    send_rims(0)
    for kind in range(2):
        for index in range(local):
            relay(0, kind, index)

    row_at = lax.broadcasted_iota(jnp.int32, (rows, width), 0)

    def neighbours(value, low, high):
        east = jnp.where(row_at == rows - 1, high, pltpu.roll(value, rows - 1, 0))
        west = jnp.where(row_at == 0, low, pltpu.roll(value, 1, 0))
        return east, west

    def slope_y(group):
        def one(index, _):
            at = group * local + index
            for part in range(2):
                for field in range(fields):
                    value = pbuf[at, part, field]
                    gy[at, part, field] = 0.5 * (
                        pltpu.roll(value, width - 1, 1) - pltpu.roll(value, 1, 1)
                    )
            return 0

        lax.fori_loop(0, local, one, 0)

    def slope_x(group):
        for index in range(local):
            at = group * local + index
            for part in range(2):
                for field in range(fields):
                    row = (index * 2 + part) * fields + field
                    east, west = neighbours(
                        pbuf[at, part, field],
                        rims[group, 0, row : row + 1, :],
                        rims[group, 1, row : row + 1, :],
                    )
                    gx[at, part, field] = 0.5 * (east - west)

    def own_terms():
        center = vbuf[...]
        east, west = neighbours(
            center,
            rims[me, 0, rim_rows : rim_rows + 1, :],
            rims[me, 1, rim_rows : rim_rows + 1, :],
        )
        east_face = 0.5 * (center + east)
        west_face = 0.5 * (center + west)
        north_face = 0.5 * (center + pltpu.roll(center, width - 1, 1))
        south_face = 0.5 * (center + pltpu.roll(center, 1, 1))
        for index in range(local):
            at = first + index
            signed = jnp.where(at < total // 2, at, at - total)
            frequency = omega_base * signed.astype(jnp.float32)
            for part in range(2):
                for field in range(fields):
                    row = (index * 2 + part) * fields + field
                    value = pbuf[at, part, field]
                    up, down = neighbours(
                        value,
                        rims[me, 0, row : row + 1, :],
                        rims[me, 1, row : row + 1, :],
                    )
                    damping = (
                        east_face * (up - value)
                        - west_face * (value - down)
                        + north_face * (pltpu.roll(value, width - 1, 1) - value)
                        - south_face * (value - pltpu.roll(value, 1, 1))
                    )
                    turned = pbuf[at, 1 - part, field] * frequency
                    result = turned - damping if part else -turned - damping
                    if field == 0 or field == 4:
                        result = result + (gx[at, part, 1] + gy[at, part, 2])
                    elif field == 1:
                        result = result + gx[at, part, 4]
                    elif field == 2:
                        result = result + gy[at, part, 4]
                    out[index, part, field] = result

    def couple(at):
        def strip(step, _):
            span = pl.ds(pl.multiple_of(step * 8, 8), 8)
            base = [[bbuf[at, part, which, span, :] for part in range(2)] for which in range(3)]
            for index in range(local):
                source = (first + index + total - at) % total
                for field in range(fields):
                    real = out[index, 0, field, span, :]
                    imag = out[index, 1, field, span, :]
                    for which, values in ((0, gx), (1, gy), (2, pbuf)):
                        a_real, a_imag = base[which]
                        q_real = values[source, 0, field, span, :]
                        q_imag = values[source, 1, field, span, :]
                        real = real + a_real * q_real - a_imag * q_imag
                        imag = imag + a_real * q_imag + a_imag * q_real
                    out[index, 0, field, span, :] = real
                    out[index, 1, field, span, :] = imag
            return 0

        lax.fori_loop(0, rows // 8, strip, 0)

    def wait_y(distance, kind, index):
        for other, what, which, copy in y_copies:
            if (other, what, which) == (distance, kind, index):
                copy.wait_recv()

    slope_y(me)
    for copy in rim_pending[0]:
        copy.wait_recv()
    relay_rims(0)
    slope_x(me)
    own_terms()
    for index in range(local):
        relays[0, 0, index].wait_recv()
    slope_y(partner)
    relays[0].wait_recv()
    slope_x(partner)

    for distance in range(1, chips):
        for index in range(local):
            wait_y(distance, 0, index)
            relay(distance, 0, index)
        pack(distance)
        send_rims(distance)
    for distance in range(1, chips):
        slope_y(group_at(distance, True))
        for index in range(local):
            relays[distance, 0, index].wait_recv()
        slope_y(group_at(distance, False))
    for distance in range(1, chips):
        for index in range(local - 1):
            wait_y(distance, 1, index)
            relay(distance, 1, index)
    for distance in range(1, chips):
        for copy in rim_pending[distance]:
            copy.wait_recv()
        relay_rims(distance)
        slope_x(group_at(distance, True))
    for distance in range(1, chips):
        relays[distance].wait_recv()
        slope_x(group_at(distance, False))

    copy_b.wait()
    for index in range(local):
        couple(first + index)
    for index in range(local):
        relays[0, 1, index].wait_recv()
        couple(partner * local + index)
    for distance in range(1, chips):
        wait_y(distance, 1, local - 1)
        relay(distance, 1, local - 1)
    for distance in range(1, chips):
        for index in range(local):
            couple(group_at(distance, True) * local + index)
    for distance in range(1, chips):
        for index in range(local):
            relays[distance, 1, index].wait_recv()
            couple(group_at(distance, False) * local + index)

    for _, _, _, copy in y_copies:
        copy.wait_send()
    for copies in rim_pending.values():
        for copy in copies:
            copy.wait_send()
    for copy in relays.values():
        copy.wait_send()


def shards(perturbation, base_flow, viscosity):
    local, parts, fields, rows, width = perturbation.shape
    groups = lax.axis_size("harm")
    tiles = lax.axis_size("tile")
    chips = groups // 2
    total = local * groups
    rim = -(-(local * parts * fields + 1) // 8) * 8
    kinds = base_flow.shape[2]
    dma = pltpu.SemaphoreType.DMA
    f32 = jnp.float32
    return pl.pallas_call(
        functools.partial(kernel, groups, tiles),
        out_shape=jax.ShapeDtypeStruct(perturbation.shape, f32),
        in_specs=[pl.BlockSpec(memory_space=pl.ANY)] * 3,
        out_specs=pl.BlockSpec(memory_space=pltpu.VMEM),
        scratch_shapes=[
            pltpu.VMEM((total, 2, fields, rows, width), f32),
            pltpu.VMEM((total, 2, kinds, rows, width), f32),
            pltpu.VMEM((rows, width), f32),
            pltpu.VMEM((chips, 2, rim, width), f32),
            pltpu.VMEM((groups, 2, rim, width), f32),
            pltpu.VMEM((total, 2, fields, rows, width), f32),
            pltpu.VMEM((total, 2, fields, rows, width), f32),
            dma((3,)),
            dma((chips - 1, 2, local)),
            dma((chips - 1, 2, local)),
            dma((chips, 2, local)),
            dma((chips, 2, local)),
            dma((chips, 2)),
            dma((chips, 2)),
            dma((chips,)),
            dma((chips,)),
        ],
        compiler_params=pltpu.CompilerParams(collective_id=0, has_side_effects=True),
    )(perturbation, base_flow, viscosity)


def solution(mesh):
    placed = (
        P("harm", None, None, ("parts", "tile"), None),
        P("harm", None, None, ("parts", "tile"), None),
        P(("parts", "tile"), None),
    )
    return jax.shard_map(
        shards,
        mesh=mesh,
        in_specs=placed,
        out_specs=P("harm", None, None, ("parts", "tile"), None),
        check_vma=False,
    )
```

time: 47.9 us -> 24.3 us (0.51)
  Pallas kernels: 0 us -> 22.4 us
  waiting for transfers between devices: 22.2 us -> 0 us
  blocking collectives: 8.61 us -> 0 us
  starting transfers between devices: 5.65 us -> 0 us
  local copies, waits for them, and re-layouts: 6.52 us -> 1.72 us
  other arithmetic: 4.13 us -> 0 us
    pallas_call x0 -> x1, Pallas kernels: none -> 22.4 us  [shards(): pl.pallas_call(functools.partial(kernel, groups, tiles), out_shape=jax.Sh...]
    ppermute x5 -> x0, waiting for transfers between devices: 22.2 us -> none  [the longest x3 22.2 us: shifted(): return lax.ppermute(value, axis, pairs)]
    all_gather x1 -> x0, blocking collectives: 8.61 us -> none  [shards(): whole_base = lax.all_gather(base_flow, 'harm', axis=0, tiled=True)]
    ppermute x5 -> x0, starting transfers between devices: 5.65 us -> none  [the longest x1 5.13 us: extended(): lax.ppermute(head, axis, [((i + 1) % count, i) for i in range(count)])]
    gather x4 -> x0, local copies, waits for them, and re-layouts: 2.3 us -> none  [block_terms(): chosen = blocks[index_table]]
    slice x10 -> x0, local copies, waits for them, and re-layouts: 1.24 us -> none  [the longest x8 1.09 us: split_rows(): grad_y = 0.5 * (jnp.roll(middle, -1, -1) - jnp.roll(middle, 1, -1))]
    reduce_sum x4 -> x0, other arithmetic: 1.12 us -> none  [block_terms(): jnp.sum(real_part, axis=1)]
    mul x10 -> x0, other arithmetic: 1.12 us -> none  [the longest x4 0.79 us: split_rows(): grad_y = 0.5 * (jnp.roll(middle, -1, -1) - jnp.roll(middle, 1, -1))]
  transfers between devices with their start and end apart: 5 -> 0, of which waited for: 3 -> 0; matrix products, arithmetic and copies ran while one was open for 6% -> 0% of each run, Pallas kernels for 0% -> 0%
where the time goes in v1:
time: 24.3 us; the launch traced here: 24.1 us
  Pallas kernels  22.4 us (92%)
  local copies, waits for them, and re-layouts  1.72 us (7%)
    pallas_call x1, Pallas kernels, shards(): pl.pallas_call(functools.partial(kernel, groups, tiles), out_shape=jax.Sh...  22.4 us
    unnamed x1, local copies, waits for them, and re-layouts  1.72 us

profile of v1, /device:TPU:0, one launch (start us, length us, event | category | flops | bytes accessed | tf_op | source)
XLA Modules:
  0.0 24.1 jit_solution(6179295683670324722)
XLA Ops:
  0.0 22.4 %shard_map.37 = f32[2,2,5,16,256]{4,3,2,1,0:T(8,128)} custom-call(f32[2,2,5,16,256]{4,3,2,1,0:T(8,128)} %p_hbm.1, f32[2,2,3,16,256]{4,3,2,1,0:T(8,128)} %b_hbm.1, f32[16,256]{1,0:T(8,128)} %v_hbm.1), custom_call_target="tpu_custom_call" | custom-call | tf_op jit(solution)/shard_map/pallas_call | solution.py:338
  22.4 1.7 %copy.5 = f32[2,2,5,16,256]{4,3,2,1,0:T(8,128)} copy(f32[2,2,5,16,256]{4,3,2,1,0:T(8,128)} %shard_map.37) | data formatting | bytes 655360

commit v2 on v1

--- a/solution.py
+++ b/solution.py
@@ -330,6 +330,8 @@
     groups = lax.axis_size("harm")
     tiles = lax.axis_size("tile")
     chips = groups // 2
+    if chips == 2 and rows % 16 == 0:
+        return halves(perturbation, base_flow, viscosity)
     total = local * groups
     rim = -(-(local * parts * fields + 1) // 8) * 8
     kinds = base_flow.shape[2]
@@ -362,6 +364,380 @@
     )(perturbation, base_flow, viscosity)
 
 
+def half_kernel(
+    groups,
+    tiles,
+    p_hbm,
+    b_hbm,
+    v_hbm,
+    out_hbm,
+    full,
+    phalf,
+    bhalf,
+    vbuf,
+    stage,
+    inner,
+    zrims,
+    edges,
+    gx,
+    gy,
+    total,
+    sent,
+    back,
+    local_sem,
+    out_sem,
+    y_send,
+    y_recv,
+    chip_send,
+    chip_recv,
+    z_send,
+    z_recv,
+    up_token,
+    down_token,
+):
+    local, _, fields, rows, width = p_hbm.shape
+    harmonics = phalf.shape[0]
+    half = rows // 2
+    rim_rows = local * 2 * fields
+    me = lax.axis_index("harm")
+    chip, core = me // 2, me % 2
+    place = lax.axis_index("tile")
+    partner = chip * 2 + (1 - core)
+    across = (1 - chip) * 2 + core
+    corner = (1 - chip) * 2 + (1 - core)
+    above, below = (place + 1) % tiles, (place + tiles - 1) % tiles
+    first = me * local
+    mine = pl.ds(pl.multiple_of(chip * half, 8), half)
+    theirs = pl.ds(pl.multiple_of((1 - chip) * half, 8), half)
+
+    def at_group(ref, group):
+        return ref.at[pl.ds(group * local, local)]
+
+    loads = [
+        pltpu.make_async_copy(source, dest, local_sem.at[at])
+        for at, (source, dest) in enumerate(
+            (
+                (p_hbm, full),
+                (v_hbm, vbuf),
+                (p_hbm.at[:, :, :, mine, :], at_group(phalf, me)),
+                (b_hbm.at[:, :, :, mine, :], at_group(bhalf, me)),
+            )
+        )
+    ]
+    for copy in loads:
+        copy.start()
+
+    barrier = pltpu.get_barrier_semaphore()
+    pl.semaphore_signal(barrier, inc=1, device_id={"harm": across}, device_id_type=MESH)
+    pl.semaphore_signal(barrier, inc=1, device_id={"harm": partner}, device_id_type=MESH)
+
+    @pl.when(place < tiles - 1)
+    def _():
+        pl.semaphore_signal(barrier, inc=1, device_id={"tile": above}, device_id_type=MESH)
+
+    @pl.when(place > 0)
+    def _():
+        pl.semaphore_signal(barrier, inc=1, device_id={"tile": below}, device_id_type=MESH)
+
+    in_line = (place < tiles - 1).astype(jnp.int32) + (place > 0).astype(jnp.int32)
+
+    loads[0].wait()
+    loads[1].wait()
+    for index in range(local):
+        for part in range(2):
+            for field in range(fields):
+                row = (index * 2 + part) * fields + field
+                span = slice(row, row + 1)
+                stage[0, span, :] = full[index, part, field, 0:1, :]
+                stage[1, span, :] = full[index, part, field, rows - 1 : rows, :]
+                edges[me, chip, span, :] = full[index, part, field, pl.ds(half - chip, 1), :]
+                inner[span, :] = full[index, part, field, pl.ds(half - 1 + chip, 1), :]
+    stage[0, rim_rows : rim_rows + 1, :] = vbuf[0:1, :]
+    stage[1, rim_rows : rim_rows + 1, :] = vbuf[rows - 1 : rows, :]
+
+    pl.semaphore_wait(barrier, 2 + in_line)
+
+    started = []
+
+    def remote(source, dest, send, recv, at, **device):
+        copy = pltpu.make_async_remote_copy(
+            src_ref=source,
+            dst_ref=dest,
+            send_sem=send.at[at],
+            recv_sem=recv.at[at],
+            device_id=device,
+            device_id_type=MESH,
+        )
+        copy.start()
+        started.append(copy)
+        return copy
+
+    def over_y(source, dest, at):
+        return remote(source, dest, y_send, y_recv, at, harm=across)
+
+    def on_chip(source, dest, at):
+        return remote(source, dest, chip_send, chip_recv, at, harm=partner)
+
+    def send_field(field):
+        return over_y(
+            p_hbm.at[:, :, field, theirs, :], at_group(phalf, me).at[:, :, field], 3 + field
+        )
+
+    early = min(3, fields)
+    y_base = over_y(b_hbm.at[:, :, :, theirs, :], at_group(bhalf, me), 0)
+    y_field = [send_field(field) for field in range(early)]
+    c_base = on_chip(b_hbm.at[:, :, :, mine, :], at_group(bhalf, me), 0)
+    c_own = on_chip(p_hbm.at[:, :, :, mine, :], at_group(phalf, me), 1)
+
+    if tiles > 2:
+
+        @pl.when(place >= 2)
+        def _():
+            pl.semaphore_wait(up_token, 1)
+
+        @pl.when((place >= 1) & (place < tiles - 1))
+        def _():
+            pl.semaphore_signal(up_token, inc=1, device_id={"tile": above}, device_id_type=MESH)
+
+        @pl.when(place <= tiles - 3)
+        def _():
+            pl.semaphore_wait(down_token, 1)
+
+        @pl.when((place >= 1) & (place < tiles - 1))
+        def _():
+            pl.semaphore_signal(down_token, inc=1, device_id={"tile": below}, device_id_type=MESH)
+
+    z_rims = [
+        remote(stage.at[0], zrims.at[0], z_send, z_recv, 1, tile=below),
+        remote(stage.at[1], zrims.at[1], z_send, z_recv, 0, tile=above),
+    ]
+
+    row_at = lax.broadcasted_iota(jnp.int32, (rows, width), 0)
+
+    def neighbours(value, high, low):
+        count = value.shape[0]
+        row = row_at[:count]
+        east = jnp.where(row == count - 1, high, pltpu.roll(value, count - 1, 0))
+        west = jnp.where(row == 0, low, pltpu.roll(value, 1, 0))
+        return east, west
+
+    def north(value):
+        return pltpu.roll(value, width - 1, 1)
+
+    def south(value):
+        return pltpu.roll(value, 1, 1)
+
+    def slopes(group, field):
+        for index in range(local):
+            at = group * local + index
+            for part in range(2):
+                row = (index * 2 + part) * fields + field
+                value = phalf[at, part, field]
+                east, west = neighbours(
+                    value, edges[group, 0, row : row + 1, :], edges[group, 1, row : row + 1, :]
+                )
+                gx[at, part, field] = 0.5 * (east - west)
+                gy[at, part, field] = 0.5 * (north(value) - south(value))
+
+    def own_terms():
+        center = vbuf[...]
+        east, west = neighbours(
+            center,
+            zrims[0, rim_rows : rim_rows + 1, :],
+            zrims[1, rim_rows : rim_rows + 1, :],
+        )
+        east_face = 0.5 * (center + east)
+        west_face = 0.5 * (center + west)
+        north_face = 0.5 * (center + north(center))
+        south_face = 0.5 * (center + south(center))
+        for index in range(local):
+            at = first + index
+            signed = jnp.where(at < harmonics // 2, at, at - harmonics)
+            frequency = omega_base * signed.astype(jnp.float32)
+            for part in range(2):
+
+                def sides(field):
+                    row = (index * 2 + part) * fields + field
+                    return neighbours(
+                        full[index, part, field],
+                        zrims[0, row : row + 1, :],
+                        zrims[1, row : row + 1, :],
+                    )
+
+                def along_x(field):
+                    up, down = sides(field)
+                    return 0.5 * (up - down)
+
+                def along_y(field):
+                    value = full[index, part, field]
+                    return 0.5 * (north(value) - south(value))
+
+                dilation = along_x(1) + along_y(2)
+                sound = {0: dilation, 4: dilation, 1: along_x(4), 2: along_y(4)}
+                for field in range(fields):
+                    value = full[index, part, field]
+                    up, down = sides(field)
+                    damping = (
+                        east_face * (up - value)
+                        - west_face * (value - down)
+                        + north_face * (north(value) - value)
+                        - south_face * (value - south(value))
+                    )
+                    turned = full[index, 1 - part, field] * frequency
+                    result = turned if part else -turned
+                    if field in sound:
+                        result = result + sound[field]
+                    total[index, part, field] = result - damping
+
+    z_rims[0].wait_recv()
+    z_rims[1].wait_recv()
+    y_outer = over_y(zrims.at[chip], edges.at[me, chip], 1)
+    y_inner = over_y(inner, edges.at[me, 1 - chip], 2)
+    y_field += [send_field(field) for field in range(early, fields)]
+    edges[me, 1 - chip] = zrims[1 - chip]
+    own_terms()
+    c_edges = on_chip(edges.at[me], edges.at[me], 2)
+
+    y_base.wait_recv()
+    c_base_across = on_chip(at_group(bhalf, across), at_group(bhalf, across), 3)
+    loads[2].wait()
+    loads[3].wait()
+    for field in range(fields):
+        slopes(me, field)
+
+    c_field = []
+
+    def relay_field(field):
+        y_field[field].wait_recv()
+        c_field.append(
+            on_chip(
+                at_group(phalf, across).at[:, :, field],
+                at_group(phalf, across).at[:, :, field],
+                5 + field,
+            )
+        )
+
+    for field in range(early):
+        relay_field(field)
+    c_own.wait_recv()
+    c_edges.wait_recv()
+    for field in range(fields):
+        slopes(partner, field)
+    y_outer.wait_recv()
+    y_inner.wait_recv()
+    c_edges_across = on_chip(edges.at[across], edges.at[across], 4)
+    c_base.wait_recv()
+    c_base_across.wait_recv()
+
+    def couple(field):
+        targets = [first + index for index in range(local)]
+        targets += [across * local + index for index in range(local)]
+
+        def step(source, sums):
+            moved = [
+                [values[source, part, field] for part in range(2)] for values in (gx, gy, phalf)
+            ]
+            after = []
+            for number, target in enumerate(targets):
+                real, imag = sums[2 * number], sums[2 * number + 1]
+                at = (target + harmonics - source) % harmonics
+                for which in range(3):
+                    a_real, a_imag = bhalf[at, 0, which], bhalf[at, 1, which]
+                    q_real, q_imag = moved[which]
+                    real = real + a_real * q_real - a_imag * q_imag
+                    imag = imag + a_real * q_imag + a_imag * q_real
+                after += [real, imag]
+            return tuple(after)
+
+        zero = jnp.zeros((half, width), jnp.float32)
+        sums = lax.fori_loop(0, harmonics, step, (zero,) * (4 * local), unroll=2)
+        for index in range(local):
+            for part in range(2):
+                sent[index, part, field] = sums[2 * (local + index) + part]
+        for index in range(local):
+            for part in range(2):
+                total[index, part, field, mine, :] += sums[2 * index + part]
+
+    def put(field, span, which):
+        copy = pltpu.make_async_copy(
+            total.at[:, :, field, span, :],
+            out_hbm.at[:, :, field, span, :],
+            out_sem.at[which, field],
+        )
+        copy.start()
+        puts.append(copy)
+
+    puts = []
+    y_back = []
+    for field in range(fields):
+        slopes(across, field)
+        if field == 0:
+            c_edges_across.wait_recv()
+        c_field[field].wait_recv()
+        slopes(corner, field)
+        couple(field)
+        y_back.append(over_y(sent.at[:, :, field], back.at[:, :, field], 3 + fields + field))
+        put(field, mine, 0)
+        if field + early < fields:
+            relay_field(field + early)
+
+    for field in range(fields):
+        y_back[field].wait_recv()
+        for index in range(local):
+            for part in range(2):
+                total[index, part, field, theirs, :] += back[index, part, field]
+        put(field, theirs, 1)
+
+    for copy in started:
+        copy.wait_send()
+    for copy in puts:
+        copy.wait()
+
+
+def halves(perturbation, base_flow, viscosity):
+    local, _, fields, rows, width = perturbation.shape
+    groups = lax.axis_size("harm")
+    tiles = lax.axis_size("tile")
+    harmonics = local * groups
+    half = rows // 2
+    rim = -(-(local * 2 * fields + 1) // 8) * 8
+    kinds = base_flow.shape[2]
+    dma = pltpu.SemaphoreType.DMA
+    f32 = jnp.float32
+    return pl.pallas_call(
+        functools.partial(half_kernel, groups, tiles),
+        out_shape=jax.ShapeDtypeStruct(perturbation.shape, f32),
+        in_specs=[pl.BlockSpec(memory_space=pl.ANY)] * 3,
+        out_specs=pl.BlockSpec(memory_space=pl.ANY),
+        scratch_shapes=[
+            pltpu.VMEM((local, 2, fields, rows, width), f32),
+            pltpu.VMEM((harmonics, 2, fields, half, width), f32),
+            pltpu.VMEM((harmonics, 2, kinds, half, width), f32),
+            pltpu.VMEM((rows, width), f32),
+            pltpu.VMEM((2, rim, width), f32),
+            pltpu.VMEM((rim, width), f32),
+            pltpu.VMEM((2, rim, width), f32),
+            pltpu.VMEM((groups, 2, rim, width), f32),
+            pltpu.VMEM((harmonics, 2, fields, half, width), f32),
+            pltpu.VMEM((harmonics, 2, fields, half, width), f32),
+            pltpu.VMEM((local, 2, fields, rows, width), f32),
+            pltpu.VMEM((local, 2, fields, half, width), f32),
+            pltpu.VMEM((local, 2, fields, half, width), f32),
+            dma((4,)),
+            dma((2, fields)),
+            dma((3 + 2 * fields,)),
+            dma((3 + 2 * fields,)),
+            dma((5 + fields,)),
+            dma((5 + fields,)),
+            dma((2,)),
+            dma((2,)),
+            pltpu.SemaphoreType.REGULAR,
+            pltpu.SemaphoreType.REGULAR,
+        ],
+        compiler_params=pltpu.CompilerParams(collective_id=0, has_side_effects=True),
+    )(perturbation, base_flow, viscosity)
+
+
 def solution(mesh):
     placed = (
         P("harm", None, None, ("parts", "tile"), None),

time: 24.3 us -> 22.4 us (0.922)
  Pallas kernels: 22.4 us -> 20.5 us
    pallas_call x1, Pallas kernels: 22.4 us -> 20.5 us  [halves(): pl.pallas_call(functools.partial(half_kernel, groups, tiles), out_shape=j...]
where the time goes in v2:
time: 22.4 us; the launch traced here: 22.2 us
  Pallas kernels  20.5 us (92%)
  local copies, waits for them, and re-layouts  1.72 us (8%)
    pallas_call x1, Pallas kernels, halves(): pl.pallas_call(functools.partial(half_kernel, groups, tiles), out_shape=j...  20.5 us
    unnamed x1, local copies, waits for them, and re-layouts  1.72 us

profile of v2, /device:TPU:0, one launch (start us, length us, event | category | flops | bytes accessed | tf_op | source)
XLA Modules:
  0.0 22.2 jit_solution(5702606601573209431)
XLA Ops:
  0.0 20.5 %shard_map.37 = f32[2,2,5,16,256]{4,3,2,1,0:T(8,128)} custom-call(f32[2,2,5,16,256]{4,3,2,1,0:T(8,128)} %p_hbm.1, f32[2,2,3,16,256]{4,3,2,1,0:T(8,128)} %b_hbm.1, f32[16,256]{1,0:T(8,128)} %v_hbm.1), custom_call_target="tpu_custom_call" | custom-call | tf_op jit(solution)/shard_map/pallas_call | solution.py:707
  20.5 1.7 %copy.5 = f32[2,2,5,16,256]{4,3,2,1,0:T(8,128)} copy(f32[2,2,5,16,256]{4,3,2,1,0:T(8,128)} %shard_map.37) | data formatting | bytes 655360

commit v3 on v2

--- a/solution.py
+++ b/solution.py
@@ -379,6 +379,10 @@
     inner,
     zrims,
     edges,
+    outer,
+    fixes,
+    fixed,
+    kept,
     gx,
     gy,
     total,
@@ -399,6 +403,7 @@
     harmonics = phalf.shape[0]
     half = rows // 2
     rim_rows = local * 2 * fields
+    rim = stage.shape[1]
     me = lax.axis_index("harm")
     chip, core = me // 2, me % 2
     place = lax.axis_index("tile")
@@ -450,7 +455,7 @@
                 span = slice(row, row + 1)
                 stage[0, span, :] = full[index, part, field, 0:1, :]
                 stage[1, span, :] = full[index, part, field, rows - 1 : rows, :]
-                edges[me, chip, span, :] = full[index, part, field, pl.ds(half - chip, 1), :]
+                edges[me, span, :] = full[index, part, field, pl.ds(half - chip, 1), :]
                 inner[span, :] = full[index, part, field, pl.ds(half - 1 + chip, 1), :]
     stage[0, rim_rows : rim_rows + 1, :] = vbuf[0:1, :]
     stage[1, rim_rows : rim_rows + 1, :] = vbuf[rows - 1 : rows, :]
@@ -483,11 +488,12 @@
             p_hbm.at[:, :, field, theirs, :], at_group(phalf, me).at[:, :, field], 3 + field
         )
 
-    early = min(3, fields)
     y_base = over_y(b_hbm.at[:, :, :, theirs, :], at_group(bhalf, me), 0)
-    y_field = [send_field(field) for field in range(early)]
+    y_inner = over_y(inner, edges.at[me], 2)
+    y_field = [send_field(field) for field in range(fields)]
     c_base = on_chip(b_hbm.at[:, :, :, mine, :], at_group(bhalf, me), 0)
     c_own = on_chip(p_hbm.at[:, :, :, mine, :], at_group(phalf, me), 1)
+    c_edges = on_chip(edges.at[me], edges.at[me], 2)
 
     if tiles > 2:
 
@@ -533,8 +539,9 @@
             for part in range(2):
                 row = (index * 2 + part) * fields + field
                 value = phalf[at, part, field]
+                inside = edges[group, row : row + 1, :]
                 east, west = neighbours(
-                    value, edges[group, 0, row : row + 1, :], edges[group, 1, row : row + 1, :]
+                    value, inside * (1 - chip).astype(inside.dtype), inside * chip.astype(inside.dtype)
                 )
                 gx[at, part, field] = 0.5 * (east - west)
                 gy[at, part, field] = 0.5 * (north(value) - south(value))
@@ -589,15 +596,6 @@
                         result = result + sound[field]
                     total[index, part, field] = result - damping
 
-    z_rims[0].wait_recv()
-    z_rims[1].wait_recv()
-    y_outer = over_y(zrims.at[chip], edges.at[me, chip], 1)
-    y_inner = over_y(inner, edges.at[me, 1 - chip], 2)
-    y_field += [send_field(field) for field in range(early, fields)]
-    edges[me, 1 - chip] = zrims[1 - chip]
-    own_terms()
-    c_edges = on_chip(edges.at[me], edges.at[me], 2)
-
     y_base.wait_recv()
     c_base_across = on_chip(at_group(bhalf, across), at_group(bhalf, across), 3)
     loads[2].wait()
@@ -617,22 +615,22 @@
             )
         )
 
-    for field in range(early):
-        relay_field(field)
+    relay_field(0)
     c_own.wait_recv()
     c_edges.wait_recv()
     for field in range(fields):
         slopes(partner, field)
-    y_outer.wait_recv()
     y_inner.wait_recv()
     c_edges_across = on_chip(edges.at[across], edges.at[across], 4)
     c_base.wait_recv()
     c_base_across.wait_recv()
+    if fields > 1:
+        relay_field(1)
+
+    targets = [first + index for index in range(local)]
+    targets += [across * local + index for index in range(local)]
 
     def couple(field):
-        targets = [first + index for index in range(local)]
-        targets += [across * local + index for index in range(local)]
-
         def step(source, sums):
             moved = [
                 [values[source, part, field] for part in range(2)] for values in (gx, gy, phalf)
@@ -656,13 +654,31 @@
                 sent[index, part, field] = sums[2 * (local + index) + part]
         for index in range(local):
             for part in range(2):
-                total[index, part, field, mine, :] += sums[2 * index + part]
-
-    def put(field, span, which):
+                kept[index, part, field] = sums[2 * index + part]
+
+    def fix():
+        edge = chip * (half - 1)
+        sign = 0.5 * (2 * chip - 1).astype(jnp.float32)
+        for number, target in enumerate(targets):
+            real = jnp.zeros((fields, width), jnp.float32)
+            imag = real
+            for group in (me, partner, across, corner):
+                for index in range(local):
+                    at = (target + harmonics - group * local - index) % harmonics
+                    a_real = sign * bhalf[at, 0, 0, pl.ds(edge, 1), :]
+                    a_imag = sign * bhalf[at, 1, 0, pl.ds(edge, 1), :]
+                    row = index * 2 * fields
+                    q_real = outer[group, row : row + fields, :]
+                    q_imag = outer[group, row + fields : row + 2 * fields, :]
+                    real = real + a_real * q_real - a_imag * q_imag
+                    imag = imag + a_real * q_imag + a_imag * q_real
+            row = number // local * rim + number % local * 2 * fields
+            fixes[row : row + fields, :] = real
+            fixes[row + fields : row + 2 * fields, :] = imag
+
+    def put(span, which):
         copy = pltpu.make_async_copy(
-            total.at[:, :, field, span, :],
-            out_hbm.at[:, :, field, span, :],
-            out_sem.at[which, field],
+            total.at[:, :, :, span, :], out_hbm.at[:, :, :, span, :], out_sem.at[which]
         )
         copy.start()
         puts.append(copy)
@@ -677,16 +693,46 @@
         slopes(corner, field)
         couple(field)
         y_back.append(over_y(sent.at[:, :, field], back.at[:, :, field], 3 + fields + field))
-        put(field, mine, 0)
-        if field + early < fields:
-            relay_field(field + early)
+        if field + 2 < fields:
+            relay_field(field + 2)
+        if field == 0:
+            z_rims[0].wait_recv()
+            z_rims[1].wait_recv()
+            y_outer = over_y(zrims.at[chip], outer.at[me], 1)
+            c_outer = on_chip(zrims.at[1 - chip], outer.at[me], 5 + fields)
+            outer[me] = zrims[1 - chip]
+            own_terms()
+        if field == min(2, fields - 1):
+            y_outer.wait_recv()
+            c_outer_across = on_chip(outer.at[across], outer.at[across], 6 + fields)
+
+    c_outer.wait_recv()
+    c_outer_across.wait_recv()
+    fix()
+    y_fix = over_y(fixes.at[rim : 2 * rim], fixed, 3 + 2 * fields)
+
+    def add_rows(rows_ref, at):
+        for index in range(local):
+            for part in range(2):
+                for field in range(fields):
+                    row = (index * 2 + part) * fields + field
+                    total[index, part, field, pl.ds(at, 1), :] += rows_ref[row : row + 1, :]
+
+    for field in range(fields):
+        for index in range(local):
+            for part in range(2):
+                total[index, part, field, mine, :] += kept[index, part, field]
+    add_rows(fixes, chip * (rows - 1))
+    put(mine, 0)
 
     for field in range(fields):
         y_back[field].wait_recv()
         for index in range(local):
             for part in range(2):
                 total[index, part, field, theirs, :] += back[index, part, field]
-        put(field, theirs, 1)
+    y_fix.wait_recv()
+    add_rows(fixed, (1 - chip) * (rows - 1))
+    put(theirs, 1)
 
     for copy in started:
         copy.wait_send()
@@ -717,18 +763,22 @@
             pltpu.VMEM((2, rim, width), f32),
             pltpu.VMEM((rim, width), f32),
             pltpu.VMEM((2, rim, width), f32),
-            pltpu.VMEM((groups, 2, rim, width), f32),
+            pltpu.VMEM((groups, rim, width), f32),
+            pltpu.VMEM((groups, rim, width), f32),
+            pltpu.VMEM((2 * rim, width), f32),
+            pltpu.VMEM((rim, width), f32),
+            pltpu.VMEM((local, 2, fields, half, width), f32),
             pltpu.VMEM((harmonics, 2, fields, half, width), f32),
             pltpu.VMEM((harmonics, 2, fields, half, width), f32),
             pltpu.VMEM((local, 2, fields, rows, width), f32),
             pltpu.VMEM((local, 2, fields, half, width), f32),
             pltpu.VMEM((local, 2, fields, half, width), f32),
             dma((4,)),
-            dma((2, fields)),
-            dma((3 + 2 * fields,)),
-            dma((3 + 2 * fields,)),
-            dma((5 + fields,)),
-            dma((5 + fields,)),
+            dma((2,)),
+            dma((4 + 2 * fields,)),
+            dma((4 + 2 * fields,)),
+            dma((7 + fields,)),
+            dma((7 + fields,)),
             dma((2,)),
             dma((2,)),
             pltpu.SemaphoreType.REGULAR,

time: 22.4 us -> 21.9 us (0.978)
  Pallas kernels: 20.5 us -> 20 us
    pallas_call x1, Pallas kernels: 20.5 us -> 20 us  [halves(): pl.pallas_call(functools.partial(half_kernel, groups, tiles), out_shape=j...]
where the time goes in v3:
time: 21.9 us; the launch traced here: 21.8 us
  Pallas kernels  20 us (91%)
  local copies, waits for them, and re-layouts  1.72 us (8%)
    pallas_call x1, Pallas kernels, halves(): pl.pallas_call(functools.partial(half_kernel, groups, tiles), out_shape=j...  20 us
    unnamed x1, local copies, waits for them, and re-layouts  1.72 us

profile of v3, /device:TPU:0, one launch (start us, length us, event | category | flops | bytes accessed | tf_op | source)
XLA Modules:
  0.0 21.8 jit_solution(18171576055661994119)
XLA Ops:
  0.0 20.0 %shard_map.37 = f32[2,2,5,16,256]{4,3,2,1,0:T(8,128)} custom-call(f32[2,2,5,16,256]{4,3,2,1,0:T(8,128)} %p_hbm.1, f32[2,2,3,16,256]{4,3,2,1,0:T(8,128)} %b_hbm.1, f32[16,256]{1,0:T(8,128)} %v_hbm.1), custom_call_target="tpu_custom_call" | custom-call | tf_op jit(solution)/shard_map/pallas_call | solution.py:753
  20.1 1.7 %copy.5 = f32[2,2,5,16,256]{4,3,2,1,0:T(8,128)} copy(f32[2,2,5,16,256]{4,3,2,1,0:T(8,128)} %shard_map.37) | data formatting | bytes 655360

commit v4 on v3

--- a/solution.py
+++ b/solution.py
@@ -620,6 +620,11 @@
     c_edges.wait_recv()
     for field in range(fields):
         slopes(partner, field)
+    z_rims[0].wait_recv()
+    z_rims[1].wait_recv()
+    y_outer = over_y(zrims.at[chip], outer.at[me], 1)
+    c_outer = on_chip(zrims.at[1 - chip], outer.at[me], 5 + fields)
+    outer[me] = zrims[1 - chip]
     y_inner.wait_recv()
     c_edges_across = on_chip(edges.at[across], edges.at[across], 4)
     c_base.wait_recv()
@@ -648,7 +653,7 @@
             return tuple(after)
 
         zero = jnp.zeros((half, width), jnp.float32)
-        sums = lax.fori_loop(0, harmonics, step, (zero,) * (4 * local), unroll=2)
+        sums = lax.fori_loop(0, harmonics, step, (zero,) * (4 * local), unroll=8)
         for index in range(local):
             for part in range(2):
                 sent[index, part, field] = sums[2 * (local + index) + part]
@@ -695,12 +700,7 @@
         y_back.append(over_y(sent.at[:, :, field], back.at[:, :, field], 3 + fields + field))
         if field + 2 < fields:
             relay_field(field + 2)
-        if field == 0:
-            z_rims[0].wait_recv()
-            z_rims[1].wait_recv()
-            y_outer = over_y(zrims.at[chip], outer.at[me], 1)
-            c_outer = on_chip(zrims.at[1 - chip], outer.at[me], 5 + fields)
-            outer[me] = zrims[1 - chip]
+        if field == 2:
             own_terms()
         if field == min(2, fields - 1):
             y_outer.wait_recv()

time: 21.9 us -> 20.7 us (0.945)
  Pallas kernels: 20 us -> 18.8 us
    pallas_call x1, Pallas kernels: 20 us -> 18.8 us  [halves(): pl.pallas_call(functools.partial(half_kernel, groups, tiles), out_shape=j...]
where the time goes in v4:
time: 20.7 us; the launch traced here: 20.5 us
  Pallas kernels  18.8 us (91%)
  local copies, waits for them, and re-layouts  1.72 us (8%)
    pallas_call x1, Pallas kernels, halves(): pl.pallas_call(functools.partial(half_kernel, groups, tiles), out_shape=j...  18.8 us
    unnamed x1, local copies, waits for them, and re-layouts  1.72 us

profile of v4, /device:TPU:0, one launch (start us, length us, event | category | flops | bytes accessed | tf_op | source)
XLA Modules:
  0.0 20.5 jit_solution(4718364152813806922)
XLA Ops:
  0.0 18.8 %shard_map.37 = f32[2,2,5,16,256]{4,3,2,1,0:T(8,128)} custom-call(f32[2,2,5,16,256]{4,3,2,1,0:T(8,128)} %p_hbm.1, f32[2,2,3,16,256]{4,3,2,1,0:T(8,128)} %b_hbm.1, f32[16,256]{1,0:T(8,128)} %v_hbm.1), custom_call_target="tpu_custom_call" | custom-call | tf_op jit(solution)/shard_map/pallas_call | solution.py:753
  18.8 1.7 %copy.5 = f32[2,2,5,16,256]{4,3,2,1,0:T(8,128)} copy(f32[2,2,5,16,256]{4,3,2,1,0:T(8,128)} %shard_map.37) | data formatting | bytes 655360
